TPU v7x, 32 devices: a whole 2x2x4 slice. The times are simulated.
32 devices in a mesh: gx: 4 (over z), gy: 8 (over y, x, core).
Axes of the slice: x: 2, y: 2, z: 4, core: 2. Of those that a mesh axis runs over, the one named last changes fastest.
Arguments:
- features: bfloat16 [32768, 256], P(('gx', 'gy')), may hold values from -6 to 6
- self_weight_one: bfloat16 [256, 256], replicated, may hold values from -0.375 to 0.375
- neigh_weight_one: bfloat16 [256, 256], replicated, may hold values from -1.5 to 1.5
- self_weight_two: bfloat16 [256, 256], replicated, may hold values from -0.375 to 0.375
- neigh_weight_two: bfloat16 [256, 256], replicated, may hold values from -1.5 to 1.5
- degree: int32 [32768], P(('gx', 'gy')), may hold values from 128 to 383
- local_tiles: bfloat16 [1024, 128, 128], P(('gx', 'gy')), may hold values from 0 to 1, as said below
- local_coord: int32 [1024, 2], P(('gx', 'gy')), may hold values from 0 to 7, as said below
- local_count: int32 [32], P(('gx', 'gy')), may hold values from 1 to 32, as said below
- send_block: int32 [256], P(('gx', 'gy')), may hold values from 0 to 7
- boundary_tiles: bfloat16 [256, 128, 128], P(('gx', 'gy')), may hold values from 0 to 1, as said below
- boundary_row: int32 [256], P(('gx', 'gy')), may hold values from 0 to 7
- hub_rows: int32 [256], P(('gx', 'gy')), may hold values from 0 to 1023
- hub_tiles: bfloat16 [256, 128, 128], P(('gx', 'gy')), may hold values from 0 to 1, as said below
- hub_coord: int32 [256, 2], P(('gx', 'gy')), may hold values from 0 to 7, as said below
Outputs:
- node_out: bfloat16 [32768, 256], P(('gx', 'gy'))
Inputs may be any that keep to these rules, and one draw needn't show every extreme that they name: `local_tiles`: entries are 0 or 1. `boundary_tiles`: entries are 0 or 1. `hub_tiles`: entries are 0 or 1. `local_coord`: both columns are row blocks of the same device. `local_count`: some device has all 32 slots live. `hub_coord`: column 0 is a row block below 8, column 1 a hub block below 2.
All inputs are finite; a program needn't handle non-finite values.
Results may differ from a plain program's by a relative error of at most 0.005.
Values may be sent and summed in bfloat16 or wider, within the bound.
A program may use at most 64 MiB of HBM per device.

v0:
```python
import jax
import jax.numpy as jnp
from jax import lax
from jax.sharding import PartitionSpec as P


def tile_sum(tiles, rows, sources, weight, block_count):
    product = jnp.einsum("kij,kjf->kif", tiles, sources, preferred_element_type=jnp.float32)
    onehot = (rows[None, :] == jnp.arange(block_count, dtype=jnp.int32)[:, None]).astype(
        jnp.float32
    ) * weight[None, :]
    flat = product.reshape(product.shape[0], -1)
    merged = jnp.dot(onehot, flat, precision=lax.Precision.HIGHEST)
    return merged.reshape(block_count, product.shape[1], product.shape[2])


def layer(
    nodes_in,
    self_weight,
    neigh_weight,
    degree,
    local_tiles,
    local_coord,
    local_count,
    send_block,
    boundary_tiles,
    boundary_row,
    hub_rows,
    hub_tiles,
    hub_coord,
):
    node_count, feat_width = nodes_in.shape
    tile_size = local_tiles.shape[1]
    block_count = node_count // tile_size
    blocks = nodes_in.reshape(block_count, tile_size, feat_width)
    own_hubs = jnp.take(nodes_in, hub_rows, axis=0)
    inner = lax.all_gather(own_hubs, "gy", axis=0, tiled=True)
    hub_feats = lax.all_gather(inner, "gx", axis=0, tiled=True)
    outgoing = jnp.take(blocks, send_block, axis=0)
    incoming = lax.all_to_all(outgoing, "gy", split_axis=0, concat_axis=0, tiled=True)
    live_mask = (jnp.arange(local_tiles.shape[0], dtype=jnp.int32) < local_count[0]).astype(
        jnp.float32
    )
    sources = jnp.take(blocks, local_coord[:, 1], axis=0)
    totals = tile_sum(local_tiles, local_coord[:, 0], sources, live_mask, block_count)
    totals = totals + tile_sum(
        boundary_tiles,
        boundary_row,
        incoming,
        jnp.ones((boundary_tiles.shape[0],), jnp.float32),
        block_count,
    )
    hub_blocks = hub_feats.reshape(-1, tile_size, feat_width)
    hub_sources = jnp.take(hub_blocks, hub_coord[:, 1], axis=0)
    totals = totals + tile_sum(
        hub_tiles,
        hub_coord[:, 0],
        hub_sources,
        jnp.ones((hub_tiles.shape[0],), jnp.float32),
        block_count,
    )
    neigh = (totals.reshape(node_count, feat_width) / degree[:, None].astype(jnp.float32)).astype(
        jnp.bfloat16
    )
    linear = jnp.dot(nodes_in, self_weight, preferred_element_type=jnp.float32)
    return linear + jnp.dot(neigh, neigh_weight, preferred_element_type=jnp.float32)


def per_device(
    features,
    self_weight_one,
    neigh_weight_one,
    self_weight_two,
    neigh_weight_two,
    degree,
    local_tiles,
    local_coord,
    local_count,
    send_block,
    boundary_tiles,
    boundary_row,
    hub_rows,
    hub_tiles,
    hub_coord,
):
    graph = (
        degree,
        local_tiles,
        local_coord,
        local_count,
        send_block,
        boundary_tiles,
        boundary_row,
        hub_rows,
        hub_tiles,
        hub_coord,
    )
    linear_one = layer(features, self_weight_one, neigh_weight_one, *graph)
    relu_one = jnp.maximum(linear_one, 0.0)
    scale = lax.rsqrt(jnp.mean(relu_one * relu_one, axis=-1, keepdims=True) + 1e-06)
    hidden = (relu_one * scale).astype(jnp.bfloat16)
    linear_two = layer(hidden, self_weight_two, neigh_weight_two, *graph)
    return linear_two.astype(jnp.bfloat16)


def solution(mesh):
    placed = (
        P(("gx", "gy"), None),
        P(),
        P(),
        P(),
        P(),
        P(("gx", "gy")),
        P(("gx", "gy"), None, None),
        P(("gx", "gy"), None),
        P(("gx", "gy")),
        P(("gx", "gy")),
        P(("gx", "gy"), None, None),
        P(("gx", "gy")),
        P(("gx", "gy")),
        P(("gx", "gy"), None, None),
        P(("gx", "gy"), None),
    )
    return jax.shard_map(
        per_device, mesh=mesh, in_specs=placed, out_specs=P(("gx", "gy"), None), check_vma=False
    )
```

profile of v0, /device:TPU:0, one launch (start us, length us, event | category | flops | bytes accessed | tf_op | source)
XLA Modules:
  0.0 126.4 jit_solution(13274462036618419214)
XLA Ops:
  0.0 0.0 copy-start
  0.0 0.8 compare_select_fusion.2
  0.8 0.7 compare_and_fusion.2
  1.5 1.6 %gather_fusion.1 = bf16[8,128,256]{2,1,0:T(8,128)(2,1)S(1)} fusion(bf16[8,128,256]{2,1,0:T(8,128)(2,1)} %bitcast.127, s32[1024]{0:T(1024)S(1)} %pad_clamp_fusion.2), kind=kCustom, calls=%fused_computation.1.clone | custom fusion | bytes 1048608 | tf_op jit(solution)/shard_map/jit(_take)/gather | solution.py:39
  3.1 0.3 copy.19
  3.4 0.9 broadcast_select_fusion.1
  4.3 0.0 copy-done.13
  4.3 5.2 %all-to-all-start = ((bf16[8,128,256]{1,2,0:T(8,128)(2,1)}), bf16[8,128,256]{1,2,0:T(8,128)(2,1)S(1)}, u32[]{:S(2)}, u32[]{:S(2)}) async-start(bf16[8,128,256]{1,2,0:T(8,128)(2,1)} %broadcast_select_fusion.1), calls=%async_computation | async-start | bytes 1048576 | tf_op jit(solution)/shard_map/all_to_all | solution.py:40
  9.5 0.6 slice_bitcast_fusion.1
  10.1 0.0 copy-done.27
  10.1 2.0 %gather_fusion = bf16[32,128,256]{2,1,0:T(8,128)(2,1)} fusion(bf16[8,128,256]{2,1,0:T(8,128)(2,1)S(1)} %bitcast.128, s32[1024]{0:T(1024)S(1)} %pad_clamp_fusion.3), kind=kCustom, calls=%fused_computation.clone | custom fusion | bytes 4194432 | tf_op jit(solution)/shard_map/jit(_take)/gather | solution.py:44
  12.2 4.4 %convolution_bitcast_fusion.1 = f32[32,128,256]{1,2,0:T(8,128)} fusion(bf16[32,128,128]{2,1,0:T(8,128)(2,1)S(1)} %copy-done, bf16[32,128,256]{2,1,0:T(8,128)(2,1)} %gather_fusion, pred[32]{0:T(512)(128)(4,1)S(1)} %get-tuple-element.10), kind=kOutput, calls=%fused_computation.15 | convolution fusion | flops 269484032 | bytes 7340064 | tf_op jit(solution)/shard_map/kij,kjf->kif/dot_general | solution.py:8
  16.6 5.4 %copy.38 = f32[4,8,128,256]{3,1,2,0:T(8,128)} copy(f32[4,8,128,256]{2,3,1,0:T(8,128)} %bitcast.130) | data formatting | bytes 8388608
  22.7 0.5 compare_convert_fusion
  23.3 0.6 gather_fusion.2
  23.8 0.0 copy-done.15
  23.8 0.1 broadcast_select_fusion.3
  23.9 9.6 %all_gather.12 = bf16[64,256]{1,0:T(8,128)(2,1)S(1)} all-gather(bf16[8,256]{1,0:T(8,128)(2,1)S(1)} %broadcast_select_fusion.3), channel_id=1, replica_groups=mesh['gx'=4,'gy'=8] {'gy'}, dimensions={0}, use_global_device_ids=true | all-gather | bytes 36864 | tf_op jit(solution)/shard_map/all_gather | solution.py:37
  33.5 13.6 %all_gather.13 = bf16[256,256]{1,0:T(8,128)(2,1)S(1)} all-gather(bf16[64,256]{1,0:T(8,128)(2,1)S(1)} %all_gather.12), channel_id=1, replica_groups=mesh['gx'=4,'gy'=8] {'gx'}, dimensions={0}, use_global_device_ids=true | all-gather | bytes 163840 | tf_op jit(solution)/shard_map/all_gather | solution.py:38
  47.1 0.5 compare_and_fusion
  47.6 1.4 %gather_fusion.3 = bf16[8,128,256]{2,1,0:T(8,128)(2,1)} fusion(bf16[2,128,256]{2,1,0:T(8,128)(2,1)S(1)} %bitcast.135, s32[1024]{0:T(1024)S(1)} %pad_clamp_fusion), kind=kCustom, calls=%fused_computation.3.clone | custom fusion | bytes 1048608 | tf_op jit(solution)/shard_map/jit(_take)/gather | solution.py:54
  49.0 1.5 %convolution_bitcast_fusion.4 = f32[8,128,256]{1,2,0:T(8,128)S(1)} fusion(bf16[8,128,128]{2,1,0:T(8,128)(2,1)} %param.36, bf16[8,128,256]{2,1,0:T(8,128)(2,1)} %gather_fusion.3, pred[8]{0:T(512)(128)(4,1)} %get-tuple-element.6), kind=kOutput, calls=%fused_computation.27 | convolution fusion | flops 67371008 | bytes 1835016 | tf_op jit(solution)/shard_map/kij,kjf->kif/dot_general | solution.py:8
  50.6 1.4 %copy.22 = f32[8,128,256]{2,1,0:T(8,128)} copy(f32[8,128,256]{1,2,0:T(8,128)S(1)} %convolution_bitcast_fusion.4) | data formatting | bytes 2097152 | tf_op jit(solution)/shard_map/kij,kjf->kif/dot_general | solution.py:8
  51.9 0.7 convert_element_type.32
  52.6 1.2 slice_bitcast_fusion
  53.8 1.3 %fusion.64 = f32[1024,256]{1,0:T(8,128)} fusion(bf16[1024,256]{1,0:T(8,128)(2,1)S(1)} %copy-done.1, bf16[256,256]{1,0:T(8,128)(2,1)S(1)} %copy-done.8), kind=kOutput, calls=%fused_computation.101 | convolution fusion | flops 134217728 | bytes 1703936 | tf_op jit(solution)/shard_map/dot_general | solution.py:65
  55.0 0.0 all-to-all-done
  55.1 0.3 convolution_bitcast_fusion.5
  55.4 1.3 %copy.20 = f32[8,128,256]{2,1,0:T(8,128)} copy(f32[8,128,256]{1,2,0:T(8,128)S(1)} %convolution_bitcast_fusion.5) | data formatting | bytes 2097152 | tf_op jit(solution)/shard_map/kij,kjf->kif/dot_general | solution.py:8
  56.7 2.5 %fusion.35 = f32[8,128,256]{2,0,1:T(8,128)S(1)} fusion(s32[8]{0:T(128)} %param.34, f32[1,8,128,256]{3,2,1,0:T(8,128)} %bitcast.131), kind=kOutput, calls=%fused_computation.64 | convolution fusion | flops 25165888 | bytes 2097184 | tf_op jit(solution)/shard_map/dot_general | solution.py:13
  59.2 3.8 %fusion.10 = f32[8,128,256]{2,0,1:T(8,128)S(1)} fusion(f32[8,128,256]{2,0,1:T(8,128)S(1)} %fusion.35, f32[32]{0:T(128)S(1)} %copy-done.21, s32[32]{0:T(128)S(1)} %copy-done.19, f32[4,8,128,256]{3,1,2,0:T(8,128)} %copy.38), kind=kOutput, calls=%fused_computation.20 | convolution fusion | flops 100925952 | bytes 6291712 | tf_op jit(solution)/shard_map/dot_general | solution.py:13
  63.0 0.0 copy-start.10
  63.1 1.2 convolution_add_fusion.3
  64.3 0.3 copy.23
  64.6 0.2 fusion.19
  64.8 0.0 copy-done.5
  64.9 0.4 multiply_reduce_fusion
  65.3 0.2 multiply_convert_fusion
  65.5 2.0 %gather_fusion.4 = bf16[32,128,256]{2,1,0:T(8,128)(2,1)} fusion(bf16[8,128,256]{2,1,0:T(8,128)(2,1)S(1)} %bitcast.125, s32[1024]{0:T(1024)S(1)} %pad_clamp_fusion.3), kind=kCustom, calls=%fused_computation.4.clone | custom fusion | bytes 4194432 | tf_op jit(solution)/shard_map/jit(_take)/gather | solution.py:44
  67.5 0.6 gather_fusion.5
  68.1 0.7 gather_fusion.6
  68.8 4.4 %convolution_bitcast_fusion = f32[32,128,256]{1,2,0:T(8,128)} fusion(bf16[32,128,128]{2,1,0:T(8,128)(2,1)S(1)} %copy-done, bf16[32,128,256]{2,1,0:T(8,128)(2,1)} %gather_fusion.4, pred[32]{0:T(512)(128)(4,1)S(1)} %copy-done.24), kind=kOutput, calls=%fused_computation.14 | convolution fusion | flops 269484032 | bytes 7340064 | tf_op jit(solution)/shard_map/kij,kjf->kif/dot_general | solution.py:8
  73.3 5.4 %copy.41 = f32[4,8,128,256]{3,1,2,0:T(8,128)} copy(f32[4,8,128,256]{2,3,1,0:T(8,128)} %bitcast.129) | data formatting | bytes 8388608
  78.7 0.3 copy.27
  79.0 0.9 broadcast_select_fusion
  79.9 3.5 %all-to-all-start.1 = ((bf16[8,128,256]{1,2,0:T(8,128)(2,1)}), bf16[8,128,256]{1,2,0:T(8,128)(2,1)S(1)}, u32[]{:S(2)}, u32[]{:S(2)}) async-start(bf16[8,128,256]{1,2,0:T(8,128)(2,1)} %broadcast_select_fusion), calls=%async_computation.1 | async-start | bytes 1048576 | tf_op jit(solution)/shard_map/all_to_all | solution.py:40
  83.4 0.1 broadcast_select_fusion.2
  83.5 12.9 %all_gather.14 = bf16[64,256]{1,0:T(8,128)(2,1)S(1)} all-gather(bf16[8,256]{1,0:T(8,128)(2,1)S(1)} %broadcast_select_fusion.2), channel_id=1, replica_groups=mesh['gx'=4,'gy'=8] {'gy'}, dimensions={0}, use_global_device_ids=true | all-gather | bytes 36864 | tf_op jit(solution)/shard_map/all_gather | solution.py:37
  96.3 13.6 %all_gather.15 = bf16[256,256]{1,0:T(8,128)(2,1)S(1)} all-gather(bf16[64,256]{1,0:T(8,128)(2,1)S(1)} %all_gather.14), channel_id=1, replica_groups=mesh['gx'=4,'gy'=8] {'gx'}, dimensions={0}, use_global_device_ids=true | all-gather | bytes 163840 | tf_op jit(solution)/shard_map/all_gather | solution.py:38
  109.9 1.4 %gather_fusion.7 = bf16[8,128,256]{2,1,0:T(8,128)(2,1)} fusion(bf16[2,128,256]{2,1,0:T(8,128)(2,1)S(1)} %bitcast.136, s32[1024]{0:T(1024)S(1)} %pad_clamp_fusion), kind=kCustom, calls=%fused_computation.7.clone | custom fusion | bytes 1048608 | tf_op jit(solution)/shard_map/jit(_take)/gather | solution.py:54
  111.3 1.5 %convolution_bitcast_fusion.2 = f32[8,128,256]{1,2,0:T(8,128)S(1)} fusion(bf16[8,128,128]{2,1,0:T(8,128)(2,1)} %param.36, bf16[8,128,256]{2,1,0:T(8,128)(2,1)} %gather_fusion.7, pred[8]{0:T(512)(128)(4,1)} %get-tuple-element.6), kind=kOutput, calls=%fused_computation.23 | convolution fusion | flops 67371008 | bytes 1835016 | tf_op jit(solution)/shard_map/kij,kjf->kif/dot_general | solution.py:8
  112.8 0.0 copy-start.12
  112.8 1.3 %copy.30 = f32[8,128,256]{2,1,0:T(8,128)} copy(f32[8,128,256]{1,2,0:T(8,128)S(1)} %convolution_bitcast_fusion.2) | data formatting | bytes 2097152 | tf_op jit(solution)/shard_map/kij,kjf->kif/dot_general | solution.py:8
  114.2 1.3 %fusion.65 = f32[1024,256]{1,0:T(8,128)} fusion(bf16[1024,256]{1,0:T(8,128)(2,1)S(1)} %multiply_convert_fusion, bf16[256,256]{1,0:T(8,128)(2,1)S(1)} %copy-done.9), kind=kOutput, calls=%fused_computation.102 | convolution fusion | flops 134217728 | bytes 1703936 | tf_op jit(solution)/shard_map/dot_general | solution.py:65
  115.5 0.0 all-to-all-done.1
  115.5 0.3 convolution_bitcast_fusion.3
  115.8 1.3 %copy.28 = f32[8,128,256]{2,1,0:T(8,128)} copy(f32[8,128,256]{1,2,0:T(8,128)S(1)} %convolution_bitcast_fusion.3) | data formatting | bytes 2097152 | tf_op jit(solution)/shard_map/kij,kjf->kif/dot_general | solution.py:8
  117.1 2.5 %fusion.33 = f32[8,128,256]{2,0,1:T(8,128)S(1)} fusion(s32[8]{0:T(128)S(1)} %copy-done.12, f32[1,8,128,256]{3,2,1,0:T(8,128)} %bitcast.132), kind=kOutput, calls=%fused_computation.63 | convolution fusion | flops 25165888 | bytes 2097184 | tf_op jit(solution)/shard_map/dot_general | solution.py:13
  119.6 3.8 %fusion.13 = f32[8,128,256]{2,0,1:T(8,128)S(1)} fusion(f32[8,128,256]{2,0,1:T(8,128)S(1)} %fusion.33, f32[32]{0:T(128)S(1)} %copy-done.22, s32[32]{0:T(128)S(1)} %copy-done.20, f32[4,8,128,256]{3,1,2,0:T(8,128)} %copy.41), kind=kOutput, calls=%fused_computation.21 | convolution fusion | flops 100925952 | bytes 6291712 | tf_op jit(solution)/shard_map/dot_general | solution.py:13
  123.5 0.0 copy-start.7
  123.5 1.2 convolution_add_fusion.2
  124.7 0.3 copy.31
  125.0 0.2 fusion.18
  125.3 1.1 fusion.17
  (56 shorter events, 0.1 us)
Async XLA Ops:
  0.0 12.2 %copy-start = (bf16[32,128,128]{2,1,0:T(8,128)(2,1)S(1)}, bf16[32,128,128]{2,1,0:T(8,128)(2,1)}, u32[]{:S(2)}) copy-start(bf16[32,128,128]{2,1,0:T(8,128)(2,1)} %param.29) | copy-start | bytes 3145732
  0.0 10.1 %copy-start.1 = (bf16[1024,256]{1,0:T(8,128)(2,1)S(1)}, bf16[1024,256]{1,0:T(8,128)(2,1)}, u32[]{:S(2)}) copy-start(bf16[1024,256]{1,0:T(8,128)(2,1)} %param.23) | copy-start | bytes 1572868
  0.0 9.5 %copy-start.25 = (s32[32,2]{0,1:T(2,128)S(1)}, s32[32,2]{0,1:T(2,128)}, u32[]{:S(2)}) copy-start(s32[32,2]{0,1:T(2,128)} %param.30) | copy-start | bytes 772
  0.0 10.1 %copy-start.27 = (s32[8]{0:T(128)S(1)}, s32[8]{0:T(128)}, u32[]{:S(2)}) copy-start(s32[8]{0:T(128)} %param.35) | copy-start | bytes 100
  1.5 2.8 %copy-start.13 = (pred[8]{0:T(512)(128)(4,1)}, pred[8]{0:T(512)(128)(4,1)S(1)}, u32[]{:S(2)}) copy-start(pred[8]{0:T(512)(128)(4,1)S(1)} %compare_and_fusion.2) | copy-start | bytes 28
  4.3 50.8 %all-to-all-start = ((bf16[8,128,256]{1,2,0:T(8,128)(2,1)}), bf16[8,128,256]{1,2,0:T(8,128)(2,1)S(1)}, u32[]{:S(2)}, u32[]{:S(2)}) async-start(bf16[8,128,256]{1,2,0:T(8,128)(2,1)} %broadcast_select_fusion.1), calls=%async_computation | async-start | bytes 1048576 | tf_op jit(solution)/shard_map/all_to_all | solution.py:40
  9.5 7.1 %copy-start.23 = (pred[32]{0:T(512)(128)(4,1)}, pred[32]{0:T(512)(128)(4,1)S(1)}, u32[]{:S(2)}) copy-start(pred[32]{0:T(512)(128)(4,1)S(1)} %get-tuple-element.10) | copy-start | bytes 100
  10.1 13.8 %copy-start.15 = (pred[8]{0:T(512)(128)(4,1)}, pred[8]{0:T(512)(128)(4,1)S(1)}, u32[]{:S(2)}) copy-start(pred[8]{0:T(512)(128)(4,1)S(1)} %compare_and_fusion.1) | copy-start | bytes 28
  16.6 30.5 %copy-start.26 = (s32[8,2]{0,1:T(2,128)S(1)}, s32[8,2]{0,1:T(2,128)}, u32[]{:S(2)}) copy-start(s32[8,2]{0,1:T(2,128)} %param.37) | copy-start | bytes 196
  22.0 31.7 %copy-start.8 = (bf16[256,256]{1,0:T(8,128)(2,1)S(1)}, bf16[256,256]{1,0:T(8,128)(2,1)}, u32[]{:S(2)}) copy-start(bf16[256,256]{1,0:T(8,128)(2,1)} %param.24) | copy-start | bytes 393220
  22.0 33.0 %copy-start.6 = (bf16[8,128,128]{2,1,0:T(8,128)(2,1)S(1)}, bf16[8,128,128]{2,1,0:T(8,128)(2,1)}, u32[]{:S(2)}) copy-start(bf16[8,128,128]{2,1,0:T(8,128)(2,1)} %param.33) | copy-start | bytes 786436
  23.3 27.3 %copy-start.11 = (s32[1024]{0:T(1024)}, s32[1024]{0:T(1024)S(1)}, u32[]{:S(2)}) copy-start(s32[1024]{0:T(1024)S(1)} %pad_clamp_fusion.1) | copy-start | bytes 12292
  55.0 4.1 %copy-start.19 = (s32[32]{0:T(128)S(1)}, s32[32]{0:T(128)}, u32[]{:S(2)}) copy-start(s32[32]{0:T(128)} %slice_bitcast_fusion.1) | copy-start | bytes 388
  55.0 4.1 %copy-start.21 = (f32[32]{0:T(128)S(1)}, f32[32]{0:T(128)}, u32[]{:S(2)}) copy-start(f32[32]{0:T(128)} %compare_convert_fusion) | copy-start | bytes 388
  56.7 6.4 %copy-start.3 = (f32[8,128,256]{2,1,0:T(8,128)S(1)}, f32[8,128,256]{2,1,0:T(8,128)}, u32[]{:S(2)}) copy-start(f32[8,128,256]{2,1,0:T(8,128)} %copy.22) | copy-start | bytes 3145732
  56.7 6.4 %copy-start.17 = (s32[8]{0:T(128)S(1)}, s32[8]{0:T(128)}, u32[]{:S(2)}) copy-start(s32[8]{0:T(128)} %slice_bitcast_fusion) | copy-start | bytes 100
  63.0 1.8 %copy-start.5 = (f32[1024,256]{1,0:T(8,128)S(1)}, f32[1024,256]{1,0:T(8,128)}, u32[]{:S(2)}) copy-start(f32[1024,256]{1,0:T(8,128)} %fusion.64) | copy-start | bytes 3145732
  63.0 1.8 %copy-start.10 = (bf16[256,256]{1,0:T(8,128)(2,1)S(1)}, bf16[256,256]{1,0:T(8,128)(2,1)}, u32[]{:S(2)}) copy-start(bf16[256,256]{1,0:T(8,128)(2,1)} %param.25) | copy-start | bytes 393220
  64.9 4.0 %copy-start.24 = (pred[32]{0:T(512)(128)(4,1)S(1)}, pred[32]{0:T(512)(128)(4,1)}, u32[]{:S(2)}) copy-start(pred[32]{0:T(512)(128)(4,1)} %copy-done.23) | copy-start | bytes 100
  73.3 5.7 %copy-start.14 = (pred[8]{0:T(512)(128)(4,1)S(1)}, pred[8]{0:T(512)(128)(4,1)}, u32[]{:S(2)}) copy-start(pred[8]{0:T(512)(128)(4,1)} %copy-done.13) | copy-start | bytes 28
  73.3 10.1 %copy-start.16 = (pred[8]{0:T(512)(128)(4,1)S(1)}, pred[8]{0:T(512)(128)(4,1)}, u32[]{:S(2)}) copy-start(pred[8]{0:T(512)(128)(4,1)} %copy-done.15) | copy-start | bytes 28
  78.7 35.5 %copy-start.9 = (bf16[256,256]{1,0:T(8,128)(2,1)S(1)}, bf16[256,256]{1,0:T(8,128)(2,1)}, u32[]{:S(2)}) copy-start(bf16[256,256]{1,0:T(8,128)(2,1)} %param.26) | copy-start | bytes 393220
  79.9 35.6 %all-to-all-start.1 = ((bf16[8,128,256]{1,2,0:T(8,128)(2,1)}), bf16[8,128,256]{1,2,0:T(8,128)(2,1)S(1)}, u32[]{:S(2)}, u32[]{:S(2)}) async-start(bf16[8,128,256]{1,2,0:T(8,128)(2,1)} %broadcast_select_fusion), calls=%async_computation.1 | async-start | bytes 1048576 | tf_op jit(solution)/shard_map/all_to_all | solution.py:40
  112.8 4.3 %copy-start.12 = (s32[8]{0:T(128)S(1)}, s32[8]{0:T(128)}, u32[]{:S(2)}) copy-start(s32[8]{0:T(128)} %param.34) | copy-start | bytes 100
  114.2 5.4 %copy-start.20 = (s32[32]{0:T(128)S(1)}, s32[32]{0:T(128)}, u32[]{:S(2)}) copy-start(s32[32]{0:T(128)} %slice_bitcast_fusion.1) | copy-start | bytes 388
  114.2 5.4 %copy-start.22 = (f32[32]{0:T(128)S(1)}, f32[32]{0:T(128)}, u32[]{:S(2)}) copy-start(f32[32]{0:T(128)} %compare_convert_fusion) | copy-start | bytes 388
  117.1 6.4 %copy-start.2 = (f32[8,128,256]{2,1,0:T(8,128)S(1)}, f32[8,128,256]{2,1,0:T(8,128)}, u32[]{:S(2)}) copy-start(f32[8,128,256]{2,1,0:T(8,128)} %copy.30) | copy-start | bytes 3145732
  117.1 6.4 %copy-start.18 = (s32[8]{0:T(128)S(1)}, s32[8]{0:T(128)}, u32[]{:S(2)}) copy-start(s32[8]{0:T(128)} %slice_bitcast_fusion) | copy-start | bytes 100
  123.4 1.8 %copy-start.4 = (f32[1024,256]{1,0:T(8,128)S(1)}, f32[1024,256]{1,0:T(8,128)}, u32[]{:S(2)}) copy-start(f32[1024,256]{1,0:T(8,128)} %fusion.65) | copy-start | bytes 3145732
  123.5 1.8 %copy-start.7 = (bf16[256,256]{1,0:T(8,128)(2,1)S(1)}, bf16[256,256]{1,0:T(8,128)(2,1)}, u32[]{:S(2)}) copy-start(bf16[256,256]{1,0:T(8,128)(2,1)} %param.27) | copy-start | bytes 393220
where the time goes:
time: 127 us; the launch traced here: 126 us
  blocking collectives  49.6 us (39%)
  matrix products  31.6 us (25%)
  local copies, waits for them, and re-layouts  29.5 us (23%)
  starting transfers between devices  8.67 us (7%)
  other arithmetic  5.83 us (5%)
    all_gather x2, blocking collectives, layer(): hub_feats = lax.all_gather(inner, 'gx', axis=0, tiled=True)  27.1 us
    all_gather x2, blocking collectives, layer(): inner = lax.all_gather(own_hubs, 'gy', axis=0, tiled=True)  22.4 us
    dot_general x6, matrix products, tile_sum(): merged = jnp.dot(onehot, flat, precision=lax.Precision.HIGHEST)  15 us
    dot_general x6, matrix products, tile_sum(): jnp.einsum('kij,kjf->kif', tiles, sources, preferred_element_type=jnp.flo...  12.5 us
    unnamed x58, local copies, waits for them, and re-layouts  11 us
    all_to_all x2, starting transfers between devices, layer(): lax.all_to_all(outgoing, 'gy', split_axis=0, concat_axis=0, tiled=True)  8.67 us
    dot_general x4, local copies, waits for them, and re-layouts, tile_sum(): jnp.einsum('kij,kjf->kif', tiles, sources, preferred_element_type=jnp.flo...  5.27 us
    gather x2, local copies, waits for them, and re-layouts, layer(): sources = jnp.take(blocks, local_coord[:, 1], axis=0)  4.08 us
  transfers between devices with their start and end apart: 2, of which 0 were waited for; matrix products, arithmetic and copies ran while one was open for 22% of the time, Pallas kernels for 0%

commit v1 on v0

--- a/solution.py
+++ b/solution.py
@@ -35,7 +35,16 @@
     blocks = nodes_in.reshape(block_count, tile_size, feat_width)
     own_hubs = jnp.take(nodes_in, hub_rows, axis=0)
     inner = lax.all_gather(own_hubs, "gy", axis=0, tiled=True)
-    hub_feats = lax.all_gather(inner, "gx", axis=0, tiled=True)
+    ways = lax.axis_size("gx")
+    up = [(d, (d + 1) % ways) for d in range(ways)]
+    down = [(d, (d - 1) % ways) for d in range(ways)]
+    earlier, later = ([inner], [inner])
+    for _ in range(ways // 2):
+        earlier.append(lax.ppermute(earlier[-1], "gx", up))
+    for _ in range((ways - 1) // 2):
+        later.append(lax.ppermute(later[-1], "gx", down))
+    line = jnp.concatenate([*earlier[::-1], *later[1:]], axis=0)
+    hub_feats = jnp.roll(line, (lax.axis_index("gx") - ways // 2) * inner.shape[0], axis=0)
     outgoing = jnp.take(blocks, send_block, axis=0)
     incoming = lax.all_to_all(outgoing, "gy", split_axis=0, concat_axis=0, tiled=True)
     live_mask = (jnp.arange(local_tiles.shape[0], dtype=jnp.int32) < local_count[0]).astype(

time: 127 us -> 97.3 us (0.77)
  blocking collectives: 49.6 us -> 20 us
  starting transfers between devices: 8.67 us -> 14.8 us
  local copies, waits for them, and re-layouts: 29.5 us -> 25.4 us
  matrix products: 31.6 us -> 28.8 us
    all_gather x2 -> x0, blocking collectives: 27.1 us -> none  [layer(): hub_feats = lax.all_gather(inner, 'gx', axis=0, tiled=True)]
    ppermute x0 -> x6, starting transfers between devices: none -> 7.76 us  [the longest x2 4.8 us: layer(): later.append(lax.ppermute(later[-1], 'gx', down))]
    dot_general x6, matrix products: 15 us -> 12.4 us  [tile_sum(): merged = jnp.dot(onehot, flat, precision=lax.Precision.HIGHEST)]
    all_gather x2, blocking collectives: 22.4 us -> 20 us  [layer(): inner = lax.all_gather(own_hubs, 'gy', axis=0, tiled=True)]
    concatenate x0 -> x2, other arithmetic: none -> 2.29 us  [layer(): jnp.roll(line, (lax.axis_index('gx') - ways // 2) * inner.shape[0], axis=0)]
    dot_general x4, local copies, waits for them, and re-layouts: 5.27 us -> 3.36 us  [tile_sum(): jnp.einsum('kij,kjf->kif', tiles, sources, preferred_element_type=jnp.flo...]
    eq x2, local copies, waits for them, and re-layouts: 1.72 us -> 0.01 us  [tile_sum(): rows[None, :] == jnp.arange(block_count, dtype=jnp.int32)[:, None]]
    all_to_all x2, starting transfers between devices: 8.67 us -> 6.99 us  [layer(): lax.all_to_all(outgoing, 'gy', split_axis=0, concat_axis=0, tiled=True)]
  transfers between devices with their start and end apart: 2 -> 8, of which waited for: 0 -> 1; matrix products, arithmetic and copies ran while one was open for 22% -> 42% of each run, Pallas kernels for 0% -> 0%
where the time goes in v1:
time: 97.3 us; the launch traced here: 96.6 us
  matrix products  28.8 us (30%)
  local copies, waits for them, and re-layouts  25.4 us (26%)
  blocking collectives  20 us (21%)
  starting transfers between devices  14.8 us (15%)
  other arithmetic  6.42 us (7%)
  between operations  1.15 us (1%)
    all_gather x2, blocking collectives, layer(): inner = lax.all_gather(own_hubs, 'gy', axis=0, tiled=True)  20 us
    dot_general x6, matrix products, tile_sum(): merged = jnp.dot(onehot, flat, precision=lax.Precision.HIGHEST)  12.4 us
    dot_general x6, matrix products, tile_sum(): jnp.einsum('kij,kjf->kif', tiles, sources, preferred_element_type=jnp.flo...  12.1 us
    unnamed x32, local copies, waits for them, and re-layouts  11.1 us
    all_to_all x2, starting transfers between devices, layer(): lax.all_to_all(outgoing, 'gy', split_axis=0, concat_axis=0, tiled=True)  6.99 us
    ppermute x2, starting transfers between devices, layer(): later.append(lax.ppermute(later[-1], 'gx', down))  4.8 us
    gather x2, local copies, waits for them, and re-layouts, layer(): sources = jnp.take(blocks, local_coord[:, 1], axis=0)  4.07 us
    dot_general x4, local copies, waits for them, and re-layouts, tile_sum(): jnp.einsum('kij,kjf->kif', tiles, sources, preferred_element_type=jnp.flo...  3.36 us
  transfers between devices with their start and end apart: 8, of which 1 were waited for; matrix products, arithmetic and copies ran while one was open for 42% of the time, Pallas kernels for 0%

profile of v1, /device:TPU:0, one launch (start us, length us, event | category | flops | bytes accessed | tf_op | source)
XLA Modules:
  0.0 96.6 jit_solution(10117655263711957254)
XLA Ops:
  0.0 0.8 compare_select_fusion.1
  0.8 0.7 compare_and_fusion.1
  1.5 1.7 %gather_fusion.2 = bf16[8,256]{1,0:T(8,128)(2,1)S(1)} fusion(bf16[1024,256]{1,0:T(8,128)(2,1)} %param.25, s32[1024]{0:T(1024)S(1)} %pad_clamp_fusion.1), kind=kCustom, calls=%fused_computation.2.clone | custom fusion | bytes 8224 | tf_op jit(solution)/shard_map/jit(_take)/gather | solution.py:36
  3.2 0.1 broadcast_select_fusion.3
  3.2 10.5 %all_gather.6 = bf16[64,256]{1,0:T(8,128)(2,1)S(1)} all-gather(bf16[8,256]{1,0:T(8,128)(2,1)S(1)} %broadcast_select_fusion.3), channel_id=1, replica_groups=mesh['gx'=4,'gy'=8] {'gy'}, dimensions={0}, use_global_device_ids=true | all-gather | bytes 36864 | tf_op jit(solution)/shard_map/all_gather | solution.py:37
  13.8 1.6 %collective-permute-start = (bf16[64,256]{1,0:T(8,128)(2,1)S(1)}, bf16[64,256]{1,0:T(8,128)(2,1)S(1)}, u32[]{:S(2)}, u32[]{:S(2)}) collective-permute-start(bf16[64,256]{1,0:T(8,128)(2,1)S(1)} %all_gather.6), channel_id=1, source_target_pairs={{0,8},{8,16},{16,24},{24,0},{1,9},{9,17},{17,25},{25,1},{2,10},{10... | collective-permute-start | bytes 98312 | tf_op jit(solution)/shard_map/ppermute | solution.py:43
  15.3 2.2 %collective-permute-start.2 = (bf16[64,256]{1,0:T(8,128)(2,1)S(1)}, bf16[64,256]{1,0:T(8,128)(2,1)S(1)}, u32[]{:S(2)}, u32[]{:S(2)}) collective-permute-start(bf16[64,256]{1,0:T(8,128)(2,1)S(1)} %all_gather.6), channel_id=1, source_target_pairs={{0,24},{8,0},{16,8},{24,16},{1,25},{9,1},{17,9},{25,17},{2,26},{10... | collective-permute-start | bytes 98312 | tf_op jit(solution)/shard_map/ppermute | solution.py:45
  17.6 1.7 %gather_fusion.1 = bf16[8,128,256]{2,1,0:T(8,128)(2,1)S(1)} fusion(bf16[8,128,256]{2,1,0:T(8,128)(2,1)} %bitcast.127, s32[1024]{0:T(1024)S(1)} %pad_clamp_fusion.2), kind=kCustom, calls=%fused_computation.1.clone | custom fusion | bytes 1048608 | tf_op jit(solution)/shard_map/jit(_take)/gather | solution.py:48
  19.3 0.3 copy.19
  19.5 0.9 broadcast_select_fusion.1
  20.5 3.5 %all-to-all-start = ((bf16[8,128,256]{1,2,0:T(8,128)(2,1)}), bf16[8,128,256]{1,2,0:T(8,128)(2,1)S(1)}, u32[]{:S(2)}, u32[]{:S(2)}) async-start(bf16[8,128,256]{1,2,0:T(8,128)(2,1)} %broadcast_select_fusion.1), calls=%async_computation | async-start | bytes 1048576 | tf_op jit(solution)/shard_map/all_to_all | solution.py:49
  24.1 2.0 %gather_fusion = bf16[32,128,256]{2,1,0:T(8,128)(2,1)} fusion(bf16[8,128,256]{2,1,0:T(8,128)(2,1)S(1)} %bitcast.128, s32[1024]{0:T(1024)S(1)} %pad_clamp_fusion.3), kind=kCustom, calls=%fused_computation.clone | custom fusion | bytes 4194432 | tf_op jit(solution)/shard_map/jit(_take)/gather | solution.py:53
  26.1 1.4 %fusion.78 = f32[1024,256]{1,0:T(8,128)} fusion(bf16[1024,256]{1,0:T(8,128)(2,1)S(1)} %copy-done.1, bf16[256,256]{1,0:T(8,128)(2,1)S(1)} %copy-done.8), kind=kOutput, calls=%fused_computation.131 | convolution fusion | flops 134217728 | bytes 1703936 | tf_op jit(solution)/shard_map/dot_general | solution.py:74
  27.5 4.4 %convolution_bitcast_fusion.1 = f32[32,128,256]{1,2,0:T(8,128)} fusion(bf16[32,128,128]{2,1,0:T(8,128)(2,1)S(1)} %copy-done, bf16[32,128,256]{2,1,0:T(8,128)(2,1)} %gather_fusion, pred[32]{0:T(512)(128)(4,1)S(1)} %get-tuple-element.10), kind=kOutput, calls=%fused_computation.15 | convolution fusion | flops 269484032 | bytes 7340064 | tf_op jit(solution)/shard_map/kij,kjf->kif/dot_general | solution.py:8
  32.5 0.1 collective-permute-start.1
  32.6 0.0 copy-start.11
  32.6 5.5 %copy.38 = f32[4,8,128,256]{3,1,2,0:T(8,128)} copy(f32[4,8,128,256]{2,3,1,0:T(8,128)} %bitcast.129) | data formatting | bytes 8388608
  38.2 0.0 collective-permute-done.2
  38.2 0.1 collective-permute-done.1
  38.3 1.1 %fusion.38 = bf16[256,256]{1,0:T(8,128)(2,1)S(1)} fusion(s32[]{:T(128)S(6)} %select_n.53, bf16[64,256]{1,0:T(8,128)(2,1)S(1)} %collective-permute-done.1, bf16[64,256]{1,0:T(8,128)(2,1)S(1)} %collective-permute-done, bf16[64,256]{1,0:T(8,128)(2,1)S(1)} %all_gather.6, bf16[64,256]{1,0:T(8,128)(2,1)S(1)} %collective-permute-done.2), kind=kLoop, calls=%fused_computation.74 | loop fusion | flops 1048576 | bytes 262148 | tf_op jit(solution)/shard_map/jit(_roll_dynamic)/concatenate | solution.py:47
  39.4 0.6 gather_fusion.3
  40.0 0.0 copy-start.12
  40.0 1.4 %convolution_bitcast_fusion.4 = f32[8,128,256]{1,2,0:T(8,128)S(1)} fusion(bf16[8,128,128]{2,1,0:T(8,128)(2,1)} %param.38, bf16[8,128,256]{2,1,0:T(8,128)(2,1)S(1)} %gather_fusion.3, pred[8]{0:T(512)(128)(4,1)S(1)} %get-tuple-element.6), kind=kOutput, calls=%fused_computation.27 | convolution fusion | flops 67371008 | bytes 1835016 | tf_op jit(solution)/shard_map/kij,kjf->kif/dot_general | solution.py:8
  41.4 1.3 %copy.22 = f32[8,128,256]{2,1,0:T(8,128)} copy(f32[8,128,256]{1,2,0:T(8,128)S(1)} %convolution_bitcast_fusion.4) | data formatting | bytes 2097152 | tf_op jit(solution)/shard_map/kij,kjf->kif/dot_general | solution.py:8
  42.8 0.0 all-to-all-done
  42.8 0.3 convolution_bitcast_fusion.5
  43.1 0.3 copy.20
  43.4 1.2 %fusion.49 = f32[8,128,256]{2,0,1:T(8,128)S(1)} fusion(s32[8]{0:T(128)S(1)} %copy-done.12, f32[1,8,128,256]{3,2,1,0:T(8,128)S(1)} %bitcast.131), kind=kOutput, calls=%fused_computation.94 | convolution fusion | flops 25165888 | bytes 2097184 | tf_op jit(solution)/shard_map/dot_general | solution.py:13
  44.6 3.8 %fusion.10 = f32[8,128,256]{2,0,1:T(8,128)S(1)} fusion(f32[8,128,256]{2,0,1:T(8,128)S(1)} %fusion.49, f32[32]{0:T(128)S(1)} %compare_convert_fusion, s32[32]{0:T(128)S(1)} %slice_bitcast_fusion.1, f32[4,8,128,256]{3,1,2,0:T(8,128)} %copy.38), kind=kOutput, calls=%fused_computation.20 | convolution fusion | flops 100925952 | bytes 6291712 | tf_op jit(solution)/shard_map/dot_general | solution.py:13
  48.5 0.0 copy-start.10
  48.5 1.2 %convolution_add_fusion.3 = f32[8,128,256]{2,0,1:T(8,128)S(1)} fusion(f32[8,128,256]{2,0,1:T(8,128)S(1)} %fusion.10, s32[8]{0:T(128)S(1)} %slice_bitcast_fusion, f32[1,8,128,256]{3,2,1,0:T(8,128)S(1)} %bitcast.134), kind=kOutput, calls=%fused_computation.30 | convolution fusion | flops 25428032 | bytes 3145760 | tf_op jit(solution)/shard_map/dot_general | solution.py:13
  49.7 0.3 copy.23
  50.0 0.2 fusion.19
  50.3 0.4 multiply_reduce_fusion
  50.7 0.2 multiply_convert_fusion
  50.9 0.6 gather_fusion.6
  51.5 0.1 broadcast_select_fusion.2
  51.6 9.4 %all_gather.7 = bf16[64,256]{1,0:T(8,128)(2,1)S(1)} all-gather(bf16[8,256]{1,0:T(8,128)(2,1)S(1)} %broadcast_select_fusion.2), channel_id=1, replica_groups=mesh['gx'=4,'gy'=8] {'gy'}, dimensions={0}, use_global_device_ids=true | all-gather | bytes 36864 | tf_op jit(solution)/shard_map/all_gather | solution.py:37
  61.0 1.3 %collective-permute-start.3 = (bf16[64,256]{1,0:T(8,128)(2,1)S(1)}, bf16[64,256]{1,0:T(8,128)(2,1)S(1)}, u32[]{:S(2)}, u32[]{:S(2)}) collective-permute-start(bf16[64,256]{1,0:T(8,128)(2,1)S(1)} %all_gather.7), channel_id=1, source_target_pairs={{0,8},{8,16},{16,24},{24,0},{1,9},{9,17},{17,25},{25,1},{2,10},{10... | collective-permute-start | bytes 98312 | tf_op jit(solution)/shard_map/ppermute | solution.py:43
  62.3 2.6 %collective-permute-start.5 = (bf16[64,256]{1,0:T(8,128)(2,1)S(1)}, bf16[64,256]{1,0:T(8,128)(2,1)S(1)}, u32[]{:S(2)}, u32[]{:S(2)}) collective-permute-start(bf16[64,256]{1,0:T(8,128)(2,1)S(1)} %all_gather.7), channel_id=1, source_target_pairs={{0,24},{8,0},{16,8},{24,16},{1,25},{9,1},{17,9},{25,17},{2,26},{10... | collective-permute-start | bytes 98312 | tf_op jit(solution)/shard_map/ppermute | solution.py:45
  64.8 2.0 %gather_fusion.4 = bf16[32,128,256]{2,1,0:T(8,128)(2,1)} fusion(bf16[8,128,256]{2,1,0:T(8,128)(2,1)S(1)} %bitcast.125, s32[1024]{0:T(1024)S(1)} %pad_clamp_fusion.3), kind=kCustom, calls=%fused_computation.4.clone | custom fusion | bytes 4194432 | tf_op jit(solution)/shard_map/jit(_take)/gather | solution.py:53
  66.9 0.6 gather_fusion.5
  67.4 0.0 copy-start.9
  67.5 4.4 %convolution_bitcast_fusion = f32[32,128,256]{1,2,0:T(8,128)} fusion(bf16[32,128,128]{2,1,0:T(8,128)(2,1)S(1)} %copy-done, bf16[32,128,256]{2,1,0:T(8,128)(2,1)} %gather_fusion.4, pred[32]{0:T(512)(128)(4,1)S(1)} %get-tuple-element.10), kind=kOutput, calls=%fused_computation.14 | convolution fusion | flops 269484032 | bytes 7340064 | tf_op jit(solution)/shard_map/kij,kjf->kif/dot_general | solution.py:8
  71.9 0.3 copy.27
  72.1 0.9 broadcast_select_fusion
  73.1 3.5 %all-to-all-start.1 = ((bf16[8,128,256]{1,2,0:T(8,128)(2,1)}), bf16[8,128,256]{1,2,0:T(8,128)(2,1)S(1)}, u32[]{:S(2)}, u32[]{:S(2)}) async-start(bf16[8,128,256]{1,2,0:T(8,128)(2,1)} %broadcast_select_fusion), calls=%async_computation.1 | async-start | bytes 1048576 | tf_op jit(solution)/shard_map/all_to_all | solution.py:49
  76.6 0.0 collective-permute-done.3
  76.6 0.1 collective-permute-start.4
  76.6 1.4 %fusion.79 = f32[1024,256]{1,0:T(8,128)} fusion(bf16[1024,256]{1,0:T(8,128)(2,1)S(1)} %multiply_convert_fusion, bf16[256,256]{1,0:T(8,128)(2,1)S(1)} %copy-done.9), kind=kOutput, calls=%fused_computation.132 | convolution fusion | flops 134217728 | bytes 1703936 | tf_op jit(solution)/shard_map/dot_general | solution.py:74
  78.0 5.5 %copy.41 = f32[4,8,128,256]{3,1,2,0:T(8,128)} copy(f32[4,8,128,256]{2,3,1,0:T(8,128)} %bitcast.130) | data formatting | bytes 8388608
  83.5 1.2 %fusion.31 = bf16[256,256]{1,0:T(8,128)(2,1)S(1)} fusion(s32[]{:T(128)S(6)} %select_n.53, bf16[64,256]{1,0:T(8,128)(2,1)S(1)} %collective-permute-done.4, bf16[64,256]{1,0:T(8,128)(2,1)S(1)} %collective-permute-done.3, bf16[64,256]{1,0:T(8,128)(2,1)S(1)} %all_gather.7, bf16[64,256]{1,0:T(8,128)(2,1)S(1)} %collective-permute-done.5), kind=kLoop, calls=%fused_computation.67 | loop fusion | flops 1048576 | bytes 262148 | tf_op jit(solution)/shard_map/jit(_roll_dynamic)/concatenate | solution.py:47
  84.7 0.6 gather_fusion.7
  85.3 1.4 %convolution_bitcast_fusion.2 = f32[8,128,256]{1,2,0:T(8,128)S(1)} fusion(bf16[8,128,128]{2,1,0:T(8,128)(2,1)} %param.38, bf16[8,128,256]{2,1,0:T(8,128)(2,1)S(1)} %gather_fusion.7, pred[8]{0:T(512)(128)(4,1)S(1)} %get-tuple-element.6), kind=kOutput, calls=%fused_computation.23 | convolution fusion | flops 67371008 | bytes 1835016 | tf_op jit(solution)/shard_map/kij,kjf->kif/dot_general | solution.py:8
  86.7 1.3 %copy.30 = f32[8,128,256]{2,1,0:T(8,128)} copy(f32[8,128,256]{1,2,0:T(8,128)S(1)} %convolution_bitcast_fusion.2) | data formatting | bytes 2097152 | tf_op jit(solution)/shard_map/kij,kjf->kif/dot_general | solution.py:8
  88.0 0.3 convolution_bitcast_fusion.3
  88.3 0.3 copy.28
  88.7 1.2 %fusion.47 = f32[8,128,256]{2,0,1:T(8,128)S(1)} fusion(s32[8]{0:T(128)S(1)} %copy-done.12, f32[1,8,128,256]{3,2,1,0:T(8,128)S(1)} %bitcast.132), kind=kOutput, calls=%fused_computation.93 | convolution fusion | flops 25165888 | bytes 2097184 | tf_op jit(solution)/shard_map/dot_general | solution.py:13
  89.9 3.8 %fusion.13 = f32[8,128,256]{2,0,1:T(8,128)S(1)} fusion(f32[8,128,256]{2,0,1:T(8,128)S(1)} %fusion.47, f32[32]{0:T(128)S(1)} %compare_convert_fusion, s32[32]{0:T(128)S(1)} %slice_bitcast_fusion.1, f32[4,8,128,256]{3,1,2,0:T(8,128)} %copy.41), kind=kOutput, calls=%fused_computation.21 | convolution fusion | flops 100925952 | bytes 6291712 | tf_op jit(solution)/shard_map/dot_general | solution.py:13
  93.7 0.0 copy-start.7
  93.7 1.2 %convolution_add_fusion.2 = f32[8,128,256]{2,0,1:T(8,128)S(1)} fusion(f32[8,128,256]{2,0,1:T(8,128)S(1)} %fusion.13, s32[8]{0:T(128)S(1)} %slice_bitcast_fusion, f32[1,8,128,256]{3,2,1,0:T(8,128)S(1)} %bitcast.133), kind=kOutput, calls=%fused_computation.29 | convolution fusion | flops 25428032 | bytes 3145760 | tf_op jit(solution)/shard_map/dot_general | solution.py:13
  94.9 0.3 copy.31
  95.3 0.2 fusion.18
  95.5 1.1 %fusion.17 = bf16[1024,256]{1,0:T(8,128)(2,1)} fusion(f32[1024,256]{1,0:T(8,128)S(1)} %copy-done.5, bf16[1024,256]{1,0:T(8,128)(2,1)S(1)} %fusion.18, bf16[256,256]{1,0:T(8,128)(2,1)S(1)} %copy-done.7), kind=kOutput, calls=%fused_computation.31 | convolution fusion | flops 134742016 | bytes 2228224 | tf_op jit(solution)/shard_map/dot_general | solution.py:75
  (40 shorter events, 0.1 us)
Async XLA Ops:
  0.0 27.5 %copy-start = (bf16[32,128,128]{2,1,0:T(8,128)(2,1)S(1)}, bf16[32,128,128]{2,1,0:T(8,128)(2,1)}, u32[]{:S(2)}) copy-start(bf16[32,128,128]{2,1,0:T(8,128)(2,1)} %param.31) | copy-start | bytes 3145732
  0.0 24.0 %copy-start.1 = (bf16[1024,256]{1,0:T(8,128)(2,1)S(1)}, bf16[1024,256]{1,0:T(8,128)(2,1)}, u32[]{:S(2)}) copy-start(bf16[1024,256]{1,0:T(8,128)(2,1)} %param.25) | copy-start | bytes 1572868
  0.0 24.0 %copy-start.13 = (s32[32,2]{0,1:T(2,128)S(1)}, s32[32,2]{0,1:T(2,128)}, u32[]{:S(2)}) copy-start(s32[32,2]{0,1:T(2,128)} %param.32) | copy-start | bytes 772
  0.0 24.0 %copy-start.14 = (s32[8,2]{0,1:T(2,128)S(1)}, s32[8,2]{0,1:T(2,128)}, u32[]{:S(2)}) copy-start(s32[8,2]{0,1:T(2,128)} %param.39) | copy-start | bytes 196
  13.8 18.7 %collective-permute-start = (bf16[64,256]{1,0:T(8,128)(2,1)S(1)}, bf16[64,256]{1,0:T(8,128)(2,1)S(1)}, u32[]{:S(2)}, u32[]{:S(2)}) collective-permute-start(bf16[64,256]{1,0:T(8,128)(2,1)S(1)} %all_gather.6), channel_id=1, source_target_pairs={{0,8},{8,16},{16,24},{24,0},{1,9},{9,17},{17,25},{25,1},{2,10},{10... | collective-permute-start | bytes 98312 | tf_op jit(solution)/shard_map/ppermute | solution.py:43
  15.3 22.8 %collective-permute-start.2 = (bf16[64,256]{1,0:T(8,128)(2,1)S(1)}, bf16[64,256]{1,0:T(8,128)(2,1)S(1)}, u32[]{:S(2)}, u32[]{:S(2)}) collective-permute-start(bf16[64,256]{1,0:T(8,128)(2,1)S(1)} %all_gather.6), channel_id=1, source_target_pairs={{0,24},{8,0},{16,8},{24,16},{1,25},{9,1},{17,9},{25,17},{2,26},{10... | collective-permute-start | bytes 98312 | tf_op jit(solution)/shard_map/ppermute | solution.py:45
  17.6 8.5 %copy-start.8 = (bf16[256,256]{1,0:T(8,128)(2,1)S(1)}, bf16[256,256]{1,0:T(8,128)(2,1)}, u32[]{:S(2)}) copy-start(bf16[256,256]{1,0:T(8,128)(2,1)} %param.26) | copy-start | bytes 393220
  20.5 22.3 %all-to-all-start = ((bf16[8,128,256]{1,2,0:T(8,128)(2,1)}), bf16[8,128,256]{1,2,0:T(8,128)(2,1)S(1)}, u32[]{:S(2)}, u32[]{:S(2)}) async-start(bf16[8,128,256]{1,2,0:T(8,128)(2,1)} %broadcast_select_fusion.1), calls=%async_computation | async-start | bytes 1048576 | tf_op jit(solution)/shard_map/all_to_all | solution.py:49
  32.5 5.8 %collective-permute-start.1 = (bf16[64,256]{1,0:T(8,128)(2,1)S(1)}, bf16[64,256]{1,0:T(8,128)(2,1)S(1)}, u32[]{:S(2)}, u32[]{:S(2)}) collective-permute-start(bf16[64,256]{1,0:T(8,128)(2,1)S(1)} %collective-permute-done), channel_id=1, source_target_pairs={{0,8},{8,16},{16,24},{24,0},{1,9},{9,17},{17,25},{25,1},{2,10},{10... | collective-permute-start | bytes 98312 | tf_op jit(solution)/shard_map/ppermute | solution.py:43
  32.6 5.6 %copy-start.11 = (s32[1024]{0:T(1024)S(1)}, s32[1024]{0:T(1024)}, u32[]{:S(2)}) copy-start(s32[1024]{0:T(1024)} %param.30) | copy-start | bytes 12292
  38.2 4.6 %copy-start.6 = (bf16[8,128,128]{2,1,0:T(8,128)(2,1)S(1)}, bf16[8,128,128]{2,1,0:T(8,128)(2,1)}, u32[]{:S(2)}) copy-start(bf16[8,128,128]{2,1,0:T(8,128)(2,1)} %param.35) | copy-start | bytes 786436
  40.0 3.4 %copy-start.12 = (s32[8]{0:T(128)S(1)}, s32[8]{0:T(128)}, u32[]{:S(2)}) copy-start(s32[8]{0:T(128)} %param.36) | copy-start | bytes 100
  43.4 5.1 %copy-start.3 = (f32[8,128,256]{2,1,0:T(8,128)S(1)}, f32[8,128,256]{2,1,0:T(8,128)}, u32[]{:S(2)}) copy-start(f32[8,128,256]{2,1,0:T(8,128)} %copy.22) | copy-start | bytes 3145732
  48.5 1.8 %copy-start.4 = (f32[1024,256]{1,0:T(8,128)S(1)}, f32[1024,256]{1,0:T(8,128)}, u32[]{:S(2)}) copy-start(f32[1024,256]{1,0:T(8,128)} %fusion.78) | copy-start | bytes 3145732
  48.5 1.8 %copy-start.10 = (bf16[256,256]{1,0:T(8,128)(2,1)S(1)}, bf16[256,256]{1,0:T(8,128)(2,1)}, u32[]{:S(2)}) copy-start(bf16[256,256]{1,0:T(8,128)(2,1)} %param.27) | copy-start | bytes 393220
  61.0 15.6 %collective-permute-start.3 = (bf16[64,256]{1,0:T(8,128)(2,1)S(1)}, bf16[64,256]{1,0:T(8,128)(2,1)S(1)}, u32[]{:S(2)}, u32[]{:S(2)}) collective-permute-start(bf16[64,256]{1,0:T(8,128)(2,1)S(1)} %all_gather.7), channel_id=1, source_target_pairs={{0,8},{8,16},{16,24},{24,0},{1,9},{9,17},{17,25},{25,1},{2,10},{10... | collective-permute-start | bytes 98312 | tf_op jit(solution)/shard_map/ppermute | solution.py:43
  62.3 21.3 %collective-permute-start.5 = (bf16[64,256]{1,0:T(8,128)(2,1)S(1)}, bf16[64,256]{1,0:T(8,128)(2,1)S(1)}, u32[]{:S(2)}, u32[]{:S(2)}) collective-permute-start(bf16[64,256]{1,0:T(8,128)(2,1)S(1)} %all_gather.7), channel_id=1, source_target_pairs={{0,24},{8,0},{16,8},{24,16},{1,25},{9,1},{17,9},{25,17},{2,26},{10... | collective-permute-start | bytes 98312 | tf_op jit(solution)/shard_map/ppermute | solution.py:45
  67.4 9.2 %copy-start.9 = (bf16[256,256]{1,0:T(8,128)(2,1)S(1)}, bf16[256,256]{1,0:T(8,128)(2,1)}, u32[]{:S(2)}) copy-start(bf16[256,256]{1,0:T(8,128)(2,1)} %param.28) | copy-start | bytes 393220
  73.1 15.0 %all-to-all-start.1 = ((bf16[8,128,256]{1,2,0:T(8,128)(2,1)}), bf16[8,128,256]{1,2,0:T(8,128)(2,1)S(1)}, u32[]{:S(2)}, u32[]{:S(2)}) async-start(bf16[8,128,256]{1,2,0:T(8,128)(2,1)} %broadcast_select_fusion), calls=%async_computation.1 | async-start | bytes 1048576 | tf_op jit(solution)/shard_map/all_to_all | solution.py:49
  76.6 7.0 %collective-permute-start.4 = (bf16[64,256]{1,0:T(8,128)(2,1)S(1)}, bf16[64,256]{1,0:T(8,128)(2,1)S(1)}, u32[]{:S(2)}, u32[]{:S(2)}) collective-permute-start(bf16[64,256]{1,0:T(8,128)(2,1)S(1)} %collective-permute-done.3), channel_id=1, source_target_pairs={{0,8},{8,16},{16,24},{24,0},{1,9},{9,17},{17,25},{25,1},{2,10},{10... | collective-permute-start | bytes 98312 | tf_op jit(solution)/shard_map/ppermute | solution.py:43
  88.7 5.1 %copy-start.2 = (f32[8,128,256]{2,1,0:T(8,128)S(1)}, f32[8,128,256]{2,1,0:T(8,128)}, u32[]{:S(2)}) copy-start(f32[8,128,256]{2,1,0:T(8,128)} %copy.30) | copy-start | bytes 3145732
  93.7 1.8 %copy-start.5 = (f32[1024,256]{1,0:T(8,128)S(1)}, f32[1024,256]{1,0:T(8,128)}, u32[]{:S(2)}) copy-start(f32[1024,256]{1,0:T(8,128)} %fusion.79) | copy-start | bytes 3145732
  93.7 1.8 %copy-start.7 = (bf16[256,256]{1,0:T(8,128)(2,1)S(1)}, bf16[256,256]{1,0:T(8,128)(2,1)}, u32[]{:S(2)}) copy-start(bf16[256,256]{1,0:T(8,128)(2,1)} %param.29) | copy-start | bytes 393220
